TPU v7x, 32 devices: a whole 2x2x4 slice. The times are simulated.
32 devices in a mesh: dp: 2 (over core), ctx: 4 (over z), vocab: 4 (over y, x).
Axes of the slice: x: 2, y: 2, z: 4, core: 2. Of those that a mesh axis runs over, the one named last changes fastest.
Arguments:
- hidden: bfloat16 [512, 4096], P(('dp', 'ctx')), may hold values from -32 to 32
- head_weight: bfloat16 [4096, 9504], P(None, ('ctx', 'vocab')), may hold values from -2 to 2
- targets: int32 [512], P('dp'), may hold values from 0 to 9503
- segment_ids: int32 [512], P('dp'), may hold values from 0 to 31, as said below
- lengths: int32 [32], replicated, may hold values from 8 to 24, as said below
- loss_mask: int32 [512], P('dp'), may hold values 0 or 1
- advantages: float32 [32], replicated, may hold values from -4 to 4
- ref_logprobs: float32 [512], P('dp'), may hold values from -40 to -2
Outputs:
- grad_hidden: bfloat16 [512, 4096], P(('dp', 'ctx', 'vocab'))
- grad_head: bfloat16 [4096, 9504], P(None, ('ctx', 'vocab'))
Inputs may be any that keep to these rules, and one draw needn't show every extreme that they name: `segment_ids`: each sequence's tokens are contiguous; the tokens b * 64 to (b + 1) * 64 - 1 carry ids b * 4 to (b + 1) * 4 - 1, never falling, each id used. lengths[s] is the number of tokens whose segment id is s.
All inputs are finite; a program needn't handle non-finite values. No bound on the sum of `loss_mask` on one device may be relied on, other than what follows from the above.
Results may differ from a plain program's by a relative error of at most 0.012.
Values may be sent and summed in bfloat16 or wider, within the bound.
A program may use at most 128 MiB of HBM per device.

v0:
```python
import jax
import jax.numpy as jnp
from jax import lax
from jax.sharding import PartitionSpec as P

LOSS_SCALE = 1024
kl_weight = 0.1
entropy_weight = 0.05


def per_device(
    hidden, head_weight, targets, segment_ids, lengths, loss_mask, advantages, ref_logprobs
):
    vocab_width = head_weight.shape[1]
    first_column = (
        lax.axis_index("ctx") * lax.axis_size("vocab") + lax.axis_index("vocab")
    ) * vocab_width
    gathered = lax.all_gather(hidden, "ctx", axis=0, tiled=True)
    logits = jnp.dot(gathered, head_weight, preferred_element_type=jnp.float32)
    columns = first_column + lax.iota(jnp.int32, vocab_width)
    target_hits = targets[:, None] == columns[None, :]
    target_part = jnp.sum(jnp.where(target_hits, logits, 0.0), axis=1)
    row_max = lax.pmax(jnp.max(logits, axis=1), ("ctx", "vocab"))
    shifted = jnp.exp(logits - row_max[:, None])
    exp_total, exp_logit, target_logit = lax.psum(
        (jnp.sum(shifted, axis=1), jnp.sum(shifted * logits, axis=1), target_part), ("ctx", "vocab")
    )
    log_total = row_max + jnp.log(exp_total)
    target_logp = target_logit - log_total
    mean_logit = exp_logit / exp_total
    probs = jnp.exp(logits - log_total[:, None])
    seq_onehot = segment_ids[:, None] == lax.iota(jnp.int32, advantages.shape[0])[None, :]
    token_adv = jnp.sum(jnp.where(seq_onehot, advantages[None, :], 0.0), axis=1)
    token_len = jnp.sum(jnp.where(seq_onehot, lengths[None, :].astype(jnp.float32), 0.0), axis=1)
    token_weight = LOSS_SCALE * loss_mask.astype(jnp.float32) / token_len
    logp_grad = -token_adv + kl_weight * (target_logp - ref_logprobs)
    inner = logp_grad[:, None] * (target_hits.astype(jnp.float32) - probs)
    inner = inner + entropy_weight * probs * (logits - mean_logit[:, None])
    grad_logits = (token_weight[:, None] * inner).astype(jnp.bfloat16)
    head_local = lax.dot_general(
        gathered, grad_logits, (((0,), (0,)), ((), ())), preferred_element_type=jnp.float32
    ).astype(jnp.bfloat16)
    grad_head = lax.psum(head_local, "dp").astype(jnp.float32).astype(jnp.bfloat16)
    grad_hidden = lax.psum_scatter(
        lax.dot_general(
            grad_logits, head_weight, (((1,), (1,)), ((), ())), preferred_element_type=jnp.float32
        ),
        ("ctx", "vocab"),
        scatter_dimension=0,
        tiled=True,
    )
    return (grad_hidden.astype(jnp.bfloat16), grad_head)


def solution(mesh):
    return jax.shard_map(
        per_device,
        mesh=mesh,
        in_specs=(
            P(("dp", "ctx"), None),
            P(None, ("ctx", "vocab")),
            P("dp"),
            P("dp"),
            P(),
            P("dp"),
            P(),
            P("dp"),
        ),
        out_specs=(P(("dp", "ctx", "vocab"), None), P(None, ("ctx", "vocab"))),
        check_vma=False,
    )
```

profile of v0, /device:TPU:0, one launch (start us, length us, event | category | flops | bytes accessed | tf_op | source)
XLA Modules:
  0.0 282.1 jit_solution(3857916356808033694)
XLA Ops:
  7.2 0.0 all-gather.2.cloned.1.call-start
  7.2 0.7 all-gather.2.cloned.1.call-update
  7.9 0.0 reduce-scatter.2.cloned.1.call-start
  7.9 0.7 convert_element_type.25
  8.6 0.8 select_reduce_fusion.1
  9.4 0.7 multiply_divide_fusion
  10.1 0.0 copy-start.1
  10.1 0.0 copy-start.2
  10.1 47.9 %all-gather.2.cloned.1.call-done = bf16[256,4096]{1,0:T(8,128)(2,1)} async-done(((bf16[64,4096]{1,0:T(8,128)(2,1)}), bf16[256,4096]{1,0:T(8,128)(2,1)}) %all-gather.2.cloned.1.call-update) | async-done | bytes 2097168 | tf_op jit(solution)/shard_map/all_gather | solution.py:18
  58.0 4.5 %fusion.11 = (f32[256]{0:T(256)S(1)}, f32[256,594]{0,1:T(8,128)S(1)}) fusion(bf16[256,4096]{1,0:T(8,128)(2,1)} %all-gather.2.cloned.1.call-done, bf16[4096,594]{0,1:T(8,128)(2,1)} %param.9), kind=kOutput, calls=%fused_computation.21 | convolution fusion | flops 1245860096 | bytes 7572480 | tf_op jit(solution)/shard_map/dot_general | solution.py:19
  62.5 39.5 %pmax.7 = f32[256]{0:T(256)S(1)} all-reduce(f32[256]{0:T(256)S(1)} %get-tuple-element.13), channel_id=1, replica_groups=mesh['dp'=2,'ctx'=4,'vocab'=4] {'ctx','vocab'}, use_global_device_ids=true, to_apply=%region_5.6 | all-reduce | flops 256 | bytes 2048 | tf_op jit(solution)/shard_map/pmax | solution.py:23
  102.0 0.0 copy-done.1
  102.0 0.2 fusion.7
  102.2 36.6 %all-reduce = (f32[256]{0:T(256)S(1)}, f32[256]{0:T(256)S(1)}, f32[256]{0:T(256)S(1)}) all-reduce(f32[256]{0:T(256)S(1)} %get-tuple-element.3, f32[256]{0:T(256)S(1)} %get-tuple-element.2, f32[256]{0:T(256)S(1)} %get-tuple-element.4), channel_id=1, replica_groups=mesh['dp'=2,'ctx'=4,'vocab'=4] {'ctx','vocab'}, use_global_device_ids=true, to_apply=%region_9.10 | all-reduce | flops 768 | bytes 6144 | tf_op jit(solution)/shard_map/psum | solution.py:25
  138.8 0.0 copy-done.2
  138.8 6.5 %fusion.9 = f32[256,4096]{1,0:T(8,128)} fusion(bf16[4096,594]{0,1:T(8,128)(2,1)} %param.9, f32[256,594]{0,1:T(8,128)S(1)} %get-tuple-element.14, f32[256]{0:T(256)S(1)} %get-tuple-element.12, f32[256]{0:T(256)S(1)} %get-tuple-element.11, f32[256]{0:T(256)S(1)} %get-tuple-element.10, s32[256]{0:T(256)S(1)} %copy-done.1, f32[256]{0:T(256)S(1)} %multiply_divide_fusion, ...), kind=kOutput, calls=%fused_computation.20 | convolution fusion | flops 1247380992 | bytes 9676104 | tf_op jit(solution)/shard_map/dot_general | solution.py:45
  145.3 0.0 copy-start
  145.3 0.0 reduce-scatter.2.cloned.1.call-update
  145.3 0.0 all-reduce.3.cloned.1.call-start
  145.4 1.5 copy-done
  146.9 3.9 %fusion = bf16[4096,594]{0,1:T(8,128)(2,1)} fusion(bf16[256,4096]{1,0:T(8,128)(2,1)S(1)} %copy-done, f32[256,594]{0,1:T(8,128)S(1)} %get-tuple-element.14, f32[256]{0:T(256)S(1)} %get-tuple-element.12, f32[256]{0:T(256)S(1)} %get-tuple-element.11, f32[256]{0:T(256)S(1)} %get-tuple-element.10, s32[256]{0:T(256)S(1)} %copy-done.1, ...), kind=kOutput, calls=%fused_computation.1 | convolution fusion | flops 1249814016 | bytes 7578952 | tf_op jit(solution)/shard_map/dot_general | solution.py:40
  150.7 0.0 all-reduce.3.cloned.1.call-update
  150.8 87.7 %reduce-scatter.2.cloned.1.call-done = f32[16,4096]{1,0:T(8,128)} async-done(((f32[256,4096]{1,0:T(8,128)}), f32[16,4096]{1,0:T(8,128)}) %reduce-scatter.2.cloned.1.call-update) | async-done | bytes 262160 | tf_op jit(solution)/shard_map/reduce_scatter | solution.py:44
  238.5 1.6 convert_element_type.28
  240.1 30.2 %all-reduce.3.cloned.1.call-done = bf16[4096,594]{0,1:T(8,128)(2,1)} async-done(((bf16[4096,594]{0,1:T(8,128)(2,1)}), bf16[4096,594]{0,1:T(8,128)(2,1)}) %all-reduce.3.cloned.1.call-update) | async-done | bytes 4866064 | tf_op jit(solution)/shard_map/psum | solution.py:43
  270.3 5.2 %copy.11 = bf16[4096,594]{0,1:T(8,128)(2,1)} copy(bf16[4096,594]{0,1:T(8,128)(2,1)} %all-reduce.3.cloned.1.call-done) | data formatting | bytes 9732096
  (2 shorter events, 0.0 us)
Async XLA Ops:
  7.2 50.8 %all-gather.2.cloned.1.call-start = ((), (), s32[]{:S(2)}) async-start(), calls=%async_computation.1 | async-start | bytes 2621440 | tf_op jit(solution)/shard_map/all_gather | solution.py:18
  7.9 230.6 %reduce-scatter.2.cloned.1.call-start = ((), (), s32[]{:S(2)}) async-start(), calls=%async_computation.2 | async-start | bytes 4456448 | tf_op jit(solution)/shard_map/reduce_scatter | solution.py:44
  10.1 91.9 %copy-start.1 = (s32[256]{0:T(256)S(1)}, s32[256]{0:T(256)}, u32[]{:S(2)}) copy-start(s32[256]{0:T(256)} %param.10) | copy-start | bytes 3076
  10.1 128.7 %copy-start.2 = (f32[256]{0:T(256)S(1)}, f32[256]{0:T(256)}, u32[]{:S(2)}) copy-start(f32[256]{0:T(256)} %param.15) | copy-start | bytes 3076
  145.3 1.6 copy-start
  145.3 125.0 %all-reduce.3.cloned.1.call-start = ((), (), s32[]{:S(2)}) async-start(), calls=%async_computation.3 | async-start | bytes 9830400 | tf_op jit(solution)/shard_map/psum | solution.py:43
Sparse Core Ops, SparseCore 0:
  9.5 48.3 all-gather.1
  145.4 93.0 reduce-scatter.1
  241.6 28.6 all-reduce.2
where the time goes:
time: 282 us
  waiting for transfers between devices  167 us (59%)
  blocking collectives  76.1 us (27%)
  matrix products  14.9 us (5%)
  between operations  13.8 us (5%)
  local copies, waits for them, and re-layouts  6.77 us (2%)
  other arithmetic  3.95 us (1%)
    reduce_scatter x1, waiting for transfers between devices, per_device(): lax.psum_scatter(lax.dot_general(grad_logits, head_weight, (((1,), (1,)),...  87.7 us
    all_gather x1, waiting for transfers between devices, per_device(): gathered = lax.all_gather(hidden, 'ctx', axis=0, tiled=True)  47.9 us
    pmax x1, blocking collectives, per_device(): row_max = lax.pmax(jnp.max(logits, axis=1), ('ctx', 'vocab'))  39.5 us
    psum x1, blocking collectives, per_device(): lax.psum((jnp.sum(shifted, axis=1), jnp.sum(shifted * logits, axis=1), ta...  36.6 us
    psum x1, waiting for transfers between devices, per_device(): lax.psum(head_local, 'dp').astype(jnp.float32).astype(jnp.bfloat16)  30.2 us
    unnamed x7, local copies, waits for them, and re-layouts  6.77 us
    dot_general x1, matrix products, per_device(): lax.dot_general(grad_logits, head_weight, (((1,), (1,)), ((), ())), prefe...  6.48 us
  transfers between devices with their start and end apart: 3, of which 3 were waited for; matrix products, arithmetic and copies ran while one was open for 3% of the time, Pallas kernels for 0%

commit v1 on v0

--- a/solution.py
+++ b/solution.py
@@ -1,3 +1,4 @@
+import functools
 import jax
 import jax.numpy as jnp
 from jax import lax
@@ -8,6 +9,14 @@
 entropy_weight = 0.05
 
 
+def draw_ways(packet, device_axis):
+    all_values = jnp.concatenate([packet for _ in range(lax.psum(1, device_axis))], axis=0)
+    return lax.all_to_all(all_values, device_axis, 0, 0, tiled=True)
+
+
+refer_the_sheets = functools.partial(draw_ways, device_axis="ctx")
+
+
 def per_device(
     hidden, head_weight, targets, segment_ids, lengths, loss_mask, advantages, ref_logprobs
 ):
@@ -15,7 +24,7 @@
     first_column = (
         lax.axis_index("ctx") * lax.axis_size("vocab") + lax.axis_index("vocab")
     ) * vocab_width
-    gathered = lax.all_gather(hidden, "ctx", axis=0, tiled=True)
+    gathered = refer_the_sheets(hidden)
     logits = jnp.dot(gathered, head_weight, preferred_element_type=jnp.float32)
     columns = first_column + lax.iota(jnp.int32, vocab_width)
     target_hits = targets[:, None] == columns[None, :]

time: 282 us -> 261 us (0.926)
  waiting for transfers between devices: 167 us -> 137 us
  starting transfers between devices: 0.12 us -> 6.39 us
    all_to_all x0 -> x1, waiting for transfers between devices: none -> 48 us  [draw_ways(): return lax.all_to_all(all_values, device_axis, 0, 0, tiled=True)]
    all_gather x1 -> x0, waiting for transfers between devices: 47.9 us -> none  [per_device(): gathered = lax.all_gather(hidden, 'ctx', axis=0, tiled=True)]
    psum x1, waiting for transfers between devices: 30.2 us -> 0.01 us  [per_device(): lax.psum(head_local, 'dp').astype(jnp.float32).astype(jnp.bfloat16)]
    all_to_all x0 -> x1, starting transfers between devices: none -> 6.35 us  [draw_ways(): return lax.all_to_all(all_values, device_axis, 0, 0, tiled=True)]
    concatenate x0 -> x1, other arithmetic: none -> 3.4 us  [draw_ways(): jnp.concatenate([packet for _ in range(lax.psum(1, device_axis))], axis=0)]
    unnamed x7 -> x13, local copies, waits for them, and re-layouts: 6.77 us -> 5.27 us
  transfers between devices with their start and end apart: 3 -> 3, of which waited for: 3 -> 2; matrix products, arithmetic and copies ran while one was open for 3% -> 2% of each run, Pallas kernels for 0% -> 0%
where the time goes in v1:
time: 261 us
  waiting for transfers between devices  137 us (52%)
  blocking collectives  76.5 us (29%)
  between operations  15.6 us (6%)
  matrix products  14.2 us (5%)
  starting transfers between devices  6.39 us (2%)
  other arithmetic  5.34 us (2%)
  local copies, waits for them, and re-layouts  5.27 us (2%)
    reduce_scatter x1, waiting for transfers between devices, per_device(): lax.psum_scatter(lax.dot_general(grad_logits, head_weight, (((1,), (1,)),...  89.3 us
    all_to_all x1, waiting for transfers between devices, draw_ways(): return lax.all_to_all(all_values, device_axis, 0, 0, tiled=True)  48 us
    pmax x1, blocking collectives, per_device(): row_max = lax.pmax(jnp.max(logits, axis=1), ('ctx', 'vocab'))  39.9 us
    psum x1, blocking collectives, per_device(): lax.psum((jnp.sum(shifted, axis=1), jnp.sum(shifted * logits, axis=1), ta...  36.6 us
    dot_general x1, matrix products, per_device(): lax.dot_general(grad_logits, head_weight, (((1,), (1,)), ((), ())), prefe...  6.47 us
    all_to_all x1, starting transfers between devices, draw_ways(): return lax.all_to_all(all_values, device_axis, 0, 0, tiled=True)  6.35 us
    unnamed x13, local copies, waits for them, and re-layouts  5.27 us
  transfers between devices with their start and end apart: 3, of which 2 were waited for; matrix products, arithmetic and copies ran while one was open for 2% of the time, Pallas kernels for 0%

profile of v1, /device:TPU:0, one launch (start us, length us, event | category | flops | bytes accessed | tf_op | source)
XLA Modules:
  0.0 260.6 jit_solution(1534828503257485814)
XLA Ops:
  8.0 0.0 copy-start.5
  8.0 0.0 copy-start.3
  8.0 0.0 copy-start.4
  8.0 0.0 copy-start.1
  8.0 3.4 %pad_maximum_fusion = bf16[256,4096]{1,0:T(8,128)(2,1)} fusion(bf16[64,4096]{1,0:T(8,128)(2,1)} %param.8), kind=kLoop, calls=%fused_computation.1 | loop fusion | flops 8388608 | bytes 2621440 | tf_op jit(solution)/shard_map/concatenate | solution.py:13
  11.4 6.3 %all-to-all-start = ((bf16[4,64,4096]{2,1,0:T(8,128)(2,1)}), bf16[4,64,4096]{2,1,0:T(8,128)(2,1)S(1)}, u32[]{:S(2)}, u32[]{:S(2)}) async-start(bf16[4,64,4096]{2,1,0:T(8,128)(2,1)} %bitcast.8), calls=%async_computation | async-start | bytes 4194304 | tf_op jit(solution)/shard_map/all_to_all | solution.py:14
  17.8 0.0 reduce-scatter.2.cloned.1.call-start
  17.8 0.0 copy-done.5
  17.8 0.0 copy-done.3
  17.8 0.0 copy-done.4
  17.8 0.1 select_reduce_fusion.1
  17.9 0.0 copy-done.1
  17.9 48.0 %all-to-all-done = bf16[4,64,4096]{2,1,0:T(8,128)(2,1)S(1)} async-done(((bf16[4,64,4096]{2,1,0:T(8,128)(2,1)}), bf16[4,64,4096]{2,1,0:T(8,128)(2,1)S(1)}, u32[]{:S(2)}, u32[]{:S(2)}) %all-to-all-start) | async-done | bytes 2097184 | tf_op jit(solution)/shard_map/all_to_all | solution.py:14
  66.0 0.0 copy-start
  66.0 0.0 copy-start.2
  66.0 3.9 %fusion.10 = (f32[256]{0:T(256)S(1)}, f32[256,594]{0,1:T(8,128)S(1)}) fusion(bf16[256,4096]{1,0:T(8,128)(2,1)S(1)} %bitcast.6, bf16[4096,594]{0,1:T(8,128)(2,1)} %param.9), kind=kOutput, calls=%fused_computation.21 | convolution fusion | flops 1245860096 | bytes 7572480 | tf_op jit(solution)/shard_map/dot_general | solution.py:28
  69.9 39.9 %pmax.7 = f32[256]{0:T(256)S(1)} all-reduce(f32[256]{0:T(256)S(1)} %get-tuple-element.13), channel_id=1, replica_groups=mesh['dp'=2,'ctx'=4,'vocab'=4] {'ctx','vocab'}, use_global_device_ids=true, to_apply=%region_5.6 | all-reduce | flops 256 | bytes 2048 | tf_op jit(solution)/shard_map/pmax | solution.py:32
  109.8 0.0 copy-done
  109.8 0.2 fusion.6
  110.0 36.6 %all-reduce = (f32[256]{0:T(256)S(1)}, f32[256]{0:T(256)S(1)}, f32[256]{0:T(256)S(1)}) all-reduce(f32[256]{0:T(256)S(1)} %get-tuple-element.3, f32[256]{0:T(256)S(1)} %get-tuple-element.2, f32[256]{0:T(256)S(1)} %get-tuple-element.4), channel_id=1, replica_groups=mesh['dp'=2,'ctx'=4,'vocab'=4] {'ctx','vocab'}, use_global_device_ids=true, to_apply=%region_9.10 | all-reduce | flops 768 | bytes 6144 | tf_op jit(solution)/shard_map/psum | solution.py:34
  146.6 0.0 copy-done.2
  146.6 6.5 %fusion.8 = f32[256,4096]{1,0:T(8,128)} fusion(bf16[4096,594]{0,1:T(8,128)(2,1)} %param.9, f32[256,594]{0,1:T(8,128)S(1)} %get-tuple-element.14, f32[256]{0:T(256)S(1)} %get-tuple-element.12, f32[256]{0:T(256)S(1)} %get-tuple-element.11, f32[256]{0:T(256)S(1)} %get-tuple-element.10, s32[256]{0:T(256)S(1)} %copy-done, f32[256]{0:T(256)S(1)} %multiply_divide_fusion, ...), kind=kOutput, calls=%fused_computation.20 | convolution fusion | flops 1247380992 | bytes 9676104 | tf_op jit(solution)/shard_map/dot_general | solution.py:54
  153.1 0.0 reduce-scatter.2.cloned.1.call-update
  153.1 0.0 all-reduce.3.cloned.1.call-start
  153.2 3.8 %convolution_convert_fusion = bf16[4096,594]{0,1:T(8,128)(2,1)} fusion(bf16[256,4096]{1,0:T(8,128)(2,1)S(1)} %bitcast.7, f32[256,594]{0,1:T(8,128)S(1)} %get-tuple-element.14, f32[256]{0:T(256)S(1)} %get-tuple-element.12, f32[256]{0:T(256)S(1)} %get-tuple-element.11, f32[256]{0:T(256)S(1)} %get-tuple-element.10, s32[256]{0:T(256)S(1)} %copy-done, ...), kind=kOutput, calls=%fused_computation | convolution fusion | flops 1249814016 | bytes 7578952 | tf_op jit(solution)/shard_map/dot_general | solution.py:49
  157.0 0.0 all-reduce.3.cloned.1.call-update
  157.0 89.3 %reduce-scatter.2.cloned.1.call-done = f32[16,4096]{1,0:T(8,128)} async-done(((f32[256,4096]{1,0:T(8,128)}), f32[16,4096]{1,0:T(8,128)}) %reduce-scatter.2.cloned.1.call-update) | async-done | bytes 262160 | tf_op jit(solution)/shard_map/reduce_scatter | solution.py:53
  246.3 1.6 convert_element_type.25
  247.9 0.0 all-reduce.3.cloned.1.call-done
  247.9 5.2 %copy.11 = bf16[4096,594]{0,1:T(8,128)(2,1)} copy(bf16[4096,594]{0,1:T(8,128)(2,1)} %all-reduce.3.cloned.1.call-done) | data formatting | bytes 9732096
  (4 shorter events, 0.0 us)
Async XLA Ops:
  8.0 9.8 %copy-start.5 = (s32[32]{0:T(128)S(1)}, s32[32]{0:T(128)}, u32[]{:S(2)}) copy-start(s32[32]{0:T(128)} %param.12) | copy-start | bytes 388
  8.0 9.8 %copy-start.3 = (s32[256]{0:T(256)S(1)}, s32[256]{0:T(256)}, u32[]{:S(2)}) copy-start(s32[256]{0:T(256)} %param.11) | copy-start | bytes 3076
  8.0 9.8 %copy-start.4 = (f32[32]{0:T(128)S(1)}, f32[32]{0:T(128)}, u32[]{:S(2)}) copy-start(f32[32]{0:T(128)} %param.14) | copy-start | bytes 388
  8.0 9.9 %copy-start.1 = (s32[256]{0:T(256)S(1)}, s32[256]{0:T(256)}, u32[]{:S(2)}) copy-start(s32[256]{0:T(256)} %param.13) | copy-start | bytes 3076
  11.4 54.5 %all-to-all-start = ((bf16[4,64,4096]{2,1,0:T(8,128)(2,1)}), bf16[4,64,4096]{2,1,0:T(8,128)(2,1)S(1)}, u32[]{:S(2)}, u32[]{:S(2)}) async-start(bf16[4,64,4096]{2,1,0:T(8,128)(2,1)} %bitcast.8), calls=%async_computation | async-start | bytes 4194304 | tf_op jit(solution)/shard_map/all_to_all | solution.py:14
  17.8 228.5 %reduce-scatter.2.cloned.1.call-start = ((), (), s32[]{:S(2)}) async-start(), calls=%async_computation.2 | async-start | bytes 4456448 | tf_op jit(solution)/shard_map/reduce_scatter | solution.py:53
  66.0 43.8 %copy-start = (s32[256]{0:T(256)S(1)}, s32[256]{0:T(256)}, u32[]{:S(2)}) copy-start(s32[256]{0:T(256)} %param.10) | copy-start | bytes 3076
  66.0 80.6 %copy-start.2 = (f32[256]{0:T(256)S(1)}, f32[256]{0:T(256)}, u32[]{:S(2)}) copy-start(f32[256]{0:T(256)} %param.15) | copy-start | bytes 3076
  153.1 94.8 %all-reduce.3.cloned.1.call-start = ((), (), s32[]{:S(2)}) async-start(), calls=%async_computation.3 | async-start | bytes 9830400 | tf_op jit(solution)/shard_map/psum | solution.py:52
Sparse Core Ops, SparseCore 0:
  153.2 93.0 reduce-scatter.1
Sparse Core Ops, SparseCore 1:
  157.1 26.3 all-reduce.2
